TPU v7x, 256 devices: a whole 4x4x8 slice. The times are simulated.
256 devices in a mesh: region: 16 (over z_lo, x, core), member: 16 (over y, z_hi).
Axes of the slice: x: 4, y: 4, z: 8 (z_hi: 4, z_lo: 2; z = z_hi * 2 + z_lo), core: 2. Of those that a mesh axis runs over, the one named last changes fastest.
Arguments:
- predicted_states: float32 [32, 100, 512, 128], P('member', None, 'region'), may hold values from -20 to 20, as said below
- observed_analysis: float32 [100, 512, 128], P(None, 'region'), may hold values from -20 to 20
- tile_location_sequence: int32 [16, 4096], P('region'), may hold values from 0 to 4095, each once within a row
Outputs:
- gradient: float32 [32, 100, 512, 128], P('member', None, 'region')
Inputs may be any that keep to these rules, and one draw needn't show every extreme that they name: Each row of tile_location_sequence is a permutation of the cells of one region. `predicted_states`: members share a common field per variable and cell, with variable and cell scales.
All inputs are finite; a program needn't handle non-finite values.
Results may differ from a plain program's by a relative error of at most 0.0003.
Values sent between devices are 32-bit elements; how exact they have to be, the bound alone decides.
A program may use at most 128 MiB of HBM per device.

v0:
```python
import jax
import jax.numpy as jnp
from jax import lax
from jax.sharding import PartitionSpec as P

LON = 128
HALF = 32
PATCH = 128


def extended(block, sides, width):
    for axis, dim in sides:
        count = lax.axis_size(axis)
        forward = [(i, i + 1) for i in range(count - 1)]
        backward = [(target, source) for source, target in forward]
        low = lax.ppermute(
            lax.slice_in_dim(block, block.shape[dim] - width, None, axis=dim), axis, forward
        )
        high = lax.ppermute(lax.slice_in_dim(block, 0, width, axis=dim), axis, backward)
        block = jnp.concatenate([low, block, high], axis=dim)
    return block


def kernel_value(offset, half):
    sigma = half / 2.0
    steps = jnp.arange(-half, half + 1).astype(jnp.float32)
    norm_sum = jnp.sum(jnp.exp(-(steps * steps) / (2.0 * sigma * sigma)))
    bell = jnp.exp(-(offset * offset) / (2.0 * sigma * sigma)) / norm_sum
    value = 0.5 * (offset == 0.0).astype(jnp.float32) + 0.5 * bell
    return jnp.where(jnp.abs(offset) <= half, value, jnp.zeros_like(value))


def lon_matrix():
    first = jnp.arange(LON)[:, None]
    second = jnp.arange(LON)[None, :]
    offset = second - first
    return kernel_value(offset.astype(jnp.float32), HALF)


def band_rows(along_lon):
    padded = extended(along_lon, (("region", 2),), HALF)
    local_rows = along_lon.shape[2]
    out_rows = jnp.arange(local_rows)[:, None]
    in_rows = jnp.arange(local_rows + 2 * HALF)[None, :]
    lat_band = kernel_value((in_rows - HALF - out_rows).astype(jnp.float32), HALF)
    return jnp.einsum("rp,mvpk->mvrk", lat_band, padded, precision=lax.Precision.HIGHEST)


def smooth_surface(values):
    along_lon = jnp.einsum("mvrl,lk->mvrk", values, lon_matrix(), precision=lax.Precision.HIGHEST)
    return band_rows(along_lon)


def pair_terms(gathered):
    members = gathered.shape[0]
    inner_products = jnp.einsum(
        "mvkp,nvkp->vkmn", gathered, gathered, precision=lax.Precision.HIGHEST
    )
    squares = jnp.einsum("mvkp,mvkp->vkm", gathered, gathered, precision=lax.Precision.HIGHEST)
    dist_sq = jnp.maximum(
        squares[:, :, :, None] + squares[:, :, None, :] - 2.0 * inner_products, 0.0
    )
    self_pair = jnp.arange(members)[:, None] == jnp.arange(members)[None, :]
    pair_weights = jnp.where(
        self_pair[None, None], jnp.zeros_like(dist_sq), 1.0 / jnp.sqrt(dist_sq + 1e-06)
    )
    pulled = jnp.transpose(jnp.sum(pair_weights, axis=-1), (2, 0, 1))
    apart = pulled[..., None] * gathered - jnp.einsum(
        "vkmn,nvkp->mvkp", pair_weights, gathered, precision=lax.Precision.HIGHEST
    )
    apart = apart / members
    return lax.all_to_all(apart, "member", split_axis=0, concat_axis=2, tiled=True)


def reorder_cells(values, positions):
    cell_count = values.shape[-1]
    flattened = values.reshape(-1, cell_count).T
    reordered = jnp.take(flattened, positions, axis=0)
    return reordered.T.reshape(values.shape)


def on_device(predicted_states, observed_analysis, tile_location_sequence):
    local_ensemble_copies = predicted_states.shape[0]
    quantity_names = predicted_states.shape[1]
    mesh_locations = predicted_states.shape[2] * predicted_states.shape[3]
    blocks = mesh_locations // PATCH
    order = tile_location_sequence[0]
    inverse_order = (
        jnp.zeros((mesh_locations,), jnp.int32).at[order].set(jnp.arange(mesh_locations))
    )
    softened_surface = smooth_surface(predicted_states)
    picked = reorder_cells(
        softened_surface.reshape(local_ensemble_copies, quantity_names, mesh_locations), order
    )
    picked = picked.reshape(local_ensemble_copies, quantity_names, blocks, PATCH)
    truth = reorder_cells(observed_analysis.reshape(quantity_names, mesh_locations), order).reshape(
        quantity_names, blocks, PATCH
    )
    diff = picked - truth[None]
    toward = diff / jnp.sqrt(jnp.sum(diff * diff, axis=-1, keepdims=True) + 1e-06)
    apart = pair_terms(lax.all_to_all(picked, "member", split_axis=2, concat_axis=0, tiled=True))
    patch_grad = jnp.sqrt(jnp.float32(PATCH)) * (toward - apart)
    located_points = reorder_cells(
        patch_grad.reshape(local_ensemble_copies, quantity_names, mesh_locations), inverse_order
    )
    return smooth_surface(located_points.reshape(predicted_states.shape))


def solution(mesh):
    in_specs = (P("member", None, "region", None), P(None, "region", None), P("region", None))
    out_specs = P("member", None, "region", None)
    return jax.shard_map(
        on_device, mesh=mesh, in_specs=in_specs, out_specs=out_specs, check_vma=False
    )
```

profile of v0, /device:TPU:1, one launch (start us, length us, event | category | flops | bytes accessed | tf_op | source)
XLA Modules:
  0.0 415.7 jit_solution(14891175216338866984)
XLA Ops:
  0.0 0.0 copy-start
  0.0 0.6 exponential_reduce_fusion
  0.6 1.3 copy-done
  1.9 5.8 %fusion.14 = f32[2,100,32,128]{3,1,2,0:T(8,128)S(1)} fusion(f32[2,100,32,128]{3,2,1,0:T(8,128)S(1)} %copy-done, f32[]{:T(128)} %exponential_reduce_fusion), kind=kOutput, calls=%fused_computation.29 | convolution fusion | flops 1258504192 | bytes 6553604 | tf_op jit(solution)/shard_map/mvrl,lk->mvrk/dot_general | solution.py:50
  7.7 0.0 copy-start.2
  7.7 0.0 copy-start.9
  7.8 0.6 copy.65
  8.4 1.0 copy-done.2
  9.4 4.5 %collective-permute-start = (f32[2,100,32,128]{3,2,1,0:T(8,128)S(1)}, f32[2,100,32,128]{3,2,1,0:T(8,128)S(1)}, u32[]{:S(2)}, u32[]{:S(2)}) collective-permute-start(f32[2,100,32,128]{3,2,1,0:T(8,128)S(1)} %copy.65), channel_id=1, source_target_pairs={{0,16},{16,32},{32,48},{48,64},{64,80},{80,96},{96,112},{112,128},... | collective-permute-start | bytes 9830408 | tf_op jit(solution)/shard_map/ppermute | solution.py:16
  13.9 2.3 collective-permute-start.1
  16.3 0.0 copy-done.9
  16.3 33.2 %collective-permute-done = f32[2,100,32,128]{3,2,1,0:T(8,128)S(1)} collective-permute-done((f32[2,100,32,128]{3,2,1,0:T(8,128)S(1)}, f32[2,100,32,128]{3,2,1,0:T(8,128)S(1)}, u32[]{:S(2)}, u32[]{:S(2)}) %collective-permute-start) | collective-permute-done | bytes 3276832 | tf_op jit(solution)/shard_map/ppermute | solution.py:16
  49.5 3.6 copy.67
  53.2 0.8 collective-permute-done.1
  53.9 3.7 copy.68
  57.7 8.5 %pad_maximum_fusion = f32[2,100,96,128]{3,1,2,0:T(8,128)} fusion(f32[2,100,32,128]{3,1,2,0:T(8,128)} %copy.68, f32[2,100,32,128]{3,1,2,0:T(8,128)} %copy-done.2, f32[2,100,32,128]{3,1,2,0:T(8,128)} %copy.67), kind=kLoop, calls=%fused_computation.4 | loop fusion | flops 4915200 | bytes 19660800 | tf_op jit(solution)/shard_map/concatenate | solution.py:20
  66.2 10.9 %fusion.6 = f32[2,100,128,32]{2,3,1,0:T(8,128)S(1)} fusion(f32[2,100,96,128]{3,1,2,0:T(8,128)} %pad_maximum_fusion, f32[]{:T(128)} %exponential_reduce_fusion, s32[96]{0:T(128)S(1)} %iota_add_fusion), kind=kOutput, calls=%fused_computation.11 | convolution fusion | flops 943758336 | bytes 13107588 | tf_op jit(solution)/shard_map/rp,mvpk->mvrk/dot_general | solution.py:46
  77.1 2.9 copy.105
  80.0 3.3 copy.70
  83.3 18.3 %gather_fusion.1 = f32[4096,200]{1,0:T(8,128)} fusion(f32[4096,200]{1,0:T(8,128)} %bitcast.86, s32[4096]{0:T(1024)S(1)} %fusion.25), kind=kCustom, calls=%fused_computation.clone | custom fusion | bytes 6569984 | tf_op jit(solution)/shard_map/jit(_take)/gather | solution.py:78
  101.6 3.7 copy.71
  105.3 0.0 copy-start.5
  105.4 1.7 copy-done.5
  107.0 0.2 select_bitcast_fusion.1
  107.3 0.6 copy.92
  107.9 0.0 copy-start.3
  107.9 4.2 %copy.74 = f32[2,100,32,128]{3,0,1,2:T(2,128)} copy(f32[2,100,32,128]{3,2,1,0:T(8,128)S(1)} %bitcast.91) | data formatting | bytes 6553600 | tf_op jit(solution)/shard_map/reshape;reshape | solution.py:95
  112.1 0.0 copy-done.3
  112.1 11.4 %all-to-all-start = ((f32[2,100,32,128]{3,0,1,2:T(2,128)}), f32[2,100,32,128]{3,0,1,2:T(2,128)S(1)}, u32[]{:S(2)}, u32[]{:S(2)}) async-start(f32[2,100,32,128]{3,0,1,2:T(2,128)} %copy.74), calls=%async_computation | async-start | bytes 6553600 | tf_op jit(solution)/shard_map/all_to_all | solution.py:101
  123.5 54.1 %all-to-all-done = f32[2,100,32,128]{3,0,1,2:T(2,128)S(1)} async-done(((f32[2,100,32,128]{3,0,1,2:T(2,128)}), f32[2,100,32,128]{3,0,1,2:T(2,128)S(1)}, u32[]{:S(2)}, u32[]{:S(2)}) %all-to-all-start) | async-done | bytes 3276832 | tf_op jit(solution)/shard_map/all_to_all | solution.py:101
  177.6 0.6 copy.75
  178.2 3.1 copy.76
  181.4 1.1 multiply_reduce_fusion
  182.5 6.2 %fusion.46 = (f32[100,2,32]{2,1,0:T(2,128)S(1)}, f32[100,2,32,32]{2,3,1,0:T(8,128)S(1)}) fusion(f32[32,100,2,128]{3,0,2,1:T(8,128)S(1)} %bitcast.89, f32[100,2,32]{2,1,0:T(2,128)S(1)} %multiply_reduce_fusion, pred[32,32]{0,1:T(8,128)(4,1)S(1)} %iota_compare_fusion), kind=kOutput, calls=%fused_computation.74 | convolution fusion | flops 316000000 | bytes 4148224 | tf_op jit(solution)/shard_map/mvkp,nvkp->vkmn/dot_general | solution.py:56
  188.7 6.6 %fusion.13 = f32[32,100,2,128]{3,0,2,1:T(8,128)S(1)} fusion(f32[32,100,2,128]{3,0,2,1:T(8,128)S(1)} %bitcast.90, f32[100,2,32,32]{2,3,1,0:T(8,128)S(1)} %get-tuple-element.7, f32[32,100,2]{0,2,1:T(2,128)S(1)} %bitcast.102), kind=kOutput, calls=%fused_computation.23 | convolution fusion | flops 317030400 | bytes 7398400 | tf_op jit(solution)/shard_map/vkmn,nvkp->mvkp/dot_general | solution.py:68
  195.3 4.2 %copy.78 = f32[32,100,2,128]{3,2,1,0:T(2,128)} copy(f32[32,100,2,128]{3,0,2,1:T(8,128)S(1)} %fusion.13) | data formatting | bytes 6553600 | tf_op jit(solution)/shard_map/div | solution.py:71
  199.6 4.5 %all-to-all-start.1 = ((f32[32,100,2,128]{3,2,1,0:T(2,128)}), f32[32,100,2,128]{3,2,1,0:T(2,128)}, u32[]{:S(2)}, u32[]{:S(2)}) async-start(f32[32,100,2,128]{3,2,1,0:T(2,128)} %copy.78), calls=%async_computation.1 | async-start | bytes 6553600 | tf_op jit(solution)/shard_map/all_to_all | solution.py:72
  204.1 1.9 copy.72
  206.0 14.1 %gather_fusion = f32[4096,100]{1,0:T(8,128)} fusion(f32[4096,100]{1,0:T(8,128)S(1)} %bitcast.87, s32[4096]{0:T(1024)S(1)} %broadcast_clamp_fusion), kind=kCustom, calls=%fused_computation.2 | custom fusion | bytes 3293184 | tf_op jit(solution)/shard_map/jit(_take)/gather | solution.py:78
  220.1 4.8 %broadcast_select_fusion = f32[4096,100]{1,0:T(8,128)} fusion(f32[4096,100]{1,0:T(8,128)} %gather_fusion, pred[4096]{0:T(1024)(128)(4,1)S(1)} %compare_and_fusion.1), kind=kLoop, calls=%fused_computation.31 | loop fusion | flops 409600 | bytes 3280896 | tf_op jit(solution)/shard_map/jit(_take)/select_n | solution.py:78
  225.0 3.0 copy.73
  228.0 15.7 %scatter_custom_fusion = s32[4096]{0:T(1024)S(1)} fusion(s32[4096]{0:T(1024)S(1)} %bitcast.106, s32[4096]{0:T(1024)S(1)} %iota.49, s32[]{:T(128)} %constant.26.clone.1), kind=kCustom, calls=%fused_computation.53 | custom fusion | bytes 16388 | tf_op jit(solution)/shard_map/scatter | solution.py:89
  243.8 2.4 multiply_reduce_fusion.1
  246.2 0.0 all-to-all-done.1
  246.2 3.8 copy.106
  250.0 4.3 %all_to_all.33 = f32[200,4096]{1,0:T(8,128)} reshape(f32[2,100,16,2,128]{4,3,2,1,0:T(2,128)S(1)} %bitcast.97) | data formatting | bytes 6553600 | tf_op jit(solution)/shard_map/all_to_all | solution.py:72
  254.3 0.9 div.56
  255.2 0.5 copy-done.7
  255.7 0.5 sub.105
  256.3 0.5 copy-done.8
  256.7 1.2 copy-done.6
  258.0 8.6 %fusion.12 = f32[4096,200]{0,1:T(8,128)} fusion(f32[200,4096]{1,0:T(8,128)S(1)} %copy-done.8, f32[25,8,32,128]{3,2,1,0:T(8,128)S(1)} %bitcast.98, f32[25,8,32,128]{3,2,1,0:T(8,128)S(1)} %bitcast.99, f32[4096,200]{0,1:T(8,128)S(1)} %copy-done.6, pred[4096]{0:T(1024)(128)(4,1)S(1)} %compare_and_fusion.1), kind=kLoop, calls=%fused_computation.19 | loop fusion | flops 4096000 | bytes 16388096 | tf_op jit(solution)/shard_map/transpose | solution.py:77
  266.6 5.2 %copy.80 = f32[4096,200]{1,0:T(8,128)} copy(f32[4096,200]{0,1:T(8,128)} %fusion.12) | data formatting | bytes 6553600 | tf_op jit(solution)/shard_map/transpose | solution.py:77
  271.8 18.3 %gather_fusion.2 = f32[4096,200]{1,0:T(8,128)} fusion(f32[4096,200]{1,0:T(8,128)} %copy.80, s32[4096]{0:T(1024)S(1)} %fusion.26), kind=kCustom, calls=%fused_computation.1.clone | custom fusion | bytes 6569984 | tf_op jit(solution)/shard_map/jit(_take)/gather | solution.py:78
  290.1 3.9 select_bitcast_fusion
  294.0 5.3 %copy.81 = f32[200,4096]{1,0:T(8,128)} copy(f32[200,4096]{0,1:T(8,128)} %select_bitcast_fusion) | data formatting | bytes 6553600 | tf_op jit(solution)/shard_map/transpose | solution.py:79
  299.3 2.5 copy.94
  301.8 3.4 fusion.20
  305.2 61.9 %collective-permute-start.2 = (f32[2,100,32,128]{3,2,1,0:T(8,128)S(1)}, f32[2,100,32,128]{3,2,1,0:T(8,128)S(1)}, u32[]{:S(2)}, u32[]{:S(2)}) collective-permute-start(f32[2,100,32,128]{3,2,1,0:T(8,128)S(1)} %fusion.20), channel_id=1, source_target_pairs={{0,16},{16,32},{32,48},{48,64},{64,80},{80,96},{96,112},{112,128},... | collective-permute-start | bytes 9830408 | tf_op jit(solution)/shard_map/ppermute | solution.py:16
  367.2 1.9 collective-permute-start.3
  369.1 33.7 %collective-permute-done.2 = f32[2,100,32,128]{3,2,1,0:T(8,128)S(1)} collective-permute-done((f32[2,100,32,128]{3,2,1,0:T(8,128)S(1)}, f32[2,100,32,128]{3,2,1,0:T(8,128)S(1)}, u32[]{:S(2)}, u32[]{:S(2)}) %collective-permute-start.2) | collective-permute-done | bytes 3276832 | tf_op jit(solution)/shard_map/ppermute | solution.py:16
  402.8 4.4 %collective-permute-done.3 = f32[2,100,32,128]{3,2,1,0:T(8,128)S(1)} collective-permute-done((f32[2,100,32,128]{3,2,1,0:T(8,128)S(1)}, f32[2,100,32,128]{3,2,1,0:T(8,128)S(1)}, u32[]{:S(2)}, u32[]{:S(2)}) %collective-permute-start.3) | collective-permute-done | bytes 3276832 | tf_op jit(solution)/shard_map/ppermute | solution.py:19
  407.2 8.0 %fusion.17 = f32[2,100,32,128]{3,2,1,0:T(8,128)} fusion(f32[2,100,32,128]{3,2,1,0:T(8,128)S(1)} %collective-permute-done.3, f32[2,100,32,128]{3,2,1,0:T(8,128)S(1)} %fusion.20, f32[2,100,32,128]{3,2,1,0:T(8,128)S(1)} %collective-permute-done.2, f32[]{:T(128)} %exponential_reduce_fusion, s32[96]{0:T(128)S(1)} %iota_add_fusion), kind=kOutput, calls=%fused_computation.30 | convolution fusion | flops 948673536 | bytes 13107588 | tf_op jit(solution)/shard_map/rp,mvpk->mvrk/dot_general | solution.py:46
  415.2 0.0 copy-done.1
  (16 shorter events, 0.1 us)
Async XLA Ops:
  0.0 1.9 copy-start
  7.7 1.7 copy-start.2
  7.7 8.5 %copy-start.9 = (s32[1,4096]{1,0:T(1,128)S(1)}, s32[1,4096]{1,0:T(1,128)}, u32[]{:S(2)}) copy-start(s32[1,4096]{1,0:T(1,128)} %param.7) | copy-start | bytes 49156
  9.4 40.1 %collective-permute-start = (f32[2,100,32,128]{3,2,1,0:T(8,128)S(1)}, f32[2,100,32,128]{3,2,1,0:T(8,128)S(1)}, u32[]{:S(2)}, u32[]{:S(2)}) collective-permute-start(f32[2,100,32,128]{3,2,1,0:T(8,128)S(1)} %copy.65), channel_id=1, source_target_pairs={{0,16},{16,32},{32,48},{48,64},{64,80},{80,96},{96,112},{112,128},... | collective-permute-start | bytes 9830408 | tf_op jit(solution)/shard_map/ppermute | solution.py:16
  13.9 40.0 %collective-permute-start.1 = (f32[2,100,32,128]{3,2,1,0:T(8,128)S(1)}, f32[2,100,32,128]{3,2,1,0:T(8,128)S(1)}, u32[]{:S(2)}, u32[]{:S(2)}) collective-permute-start(f32[2,100,32,128]{3,2,1,0:T(8,128)S(1)} %copy.65), channel_id=1, source_target_pairs={{16,0},{32,16},{48,32},{64,48},{80,64},{96,80},{112,96},{128,112},... | collective-permute-start | bytes 9830408 | tf_op jit(solution)/shard_map/ppermute | solution.py:19
  105.3 1.7 copy-start.5
  107.9 4.2 %copy-start.3 = (f32[25,8,32,128]{3,2,1,0:T(8,128)}, f32[25,8,32,128]{3,2,1,0:T(8,128)S(1)}, u32[]{:S(2)}) copy-start(f32[25,8,32,128]{3,2,1,0:T(8,128)S(1)} %copy.92) | copy-start | bytes 9830404
  112.1 65.5 %all-to-all-start = ((f32[2,100,32,128]{3,0,1,2:T(2,128)}), f32[2,100,32,128]{3,0,1,2:T(2,128)S(1)}, u32[]{:S(2)}, u32[]{:S(2)}) async-start(f32[2,100,32,128]{3,0,1,2:T(2,128)} %copy.74), calls=%async_computation | async-start | bytes 6553600 | tf_op jit(solution)/shard_map/all_to_all | solution.py:101
  199.6 46.6 %all-to-all-start.1 = ((f32[32,100,2,128]{3,2,1,0:T(2,128)}), f32[32,100,2,128]{3,2,1,0:T(2,128)}, u32[]{:S(2)}, u32[]{:S(2)}) async-start(f32[32,100,2,128]{3,2,1,0:T(2,128)} %copy.78), calls=%async_computation.1 | async-start | bytes 6553600 | tf_op jit(solution)/shard_map/all_to_all | solution.py:72
  220.1 23.6 %copy-start.4 = (f32[25,8,32,128]{3,2,1,0:T(8,128)S(1)}, f32[25,8,32,128]{3,2,1,0:T(8,128)}, u32[]{:S(2)}) copy-start(f32[25,8,32,128]{3,2,1,0:T(8,128)} %copy-done.3) | copy-start | bytes 9830404
  254.3 1.4 copy-start.7
  254.3 2.4 copy-start.8
  255.2 2.7 copy-start.6
  305.2 97.5 %collective-permute-start.2 = (f32[2,100,32,128]{3,2,1,0:T(8,128)S(1)}, f32[2,100,32,128]{3,2,1,0:T(8,128)S(1)}, u32[]{:S(2)}, u32[]{:S(2)}) collective-permute-start(f32[2,100,32,128]{3,2,1,0:T(8,128)S(1)} %fusion.20), channel_id=1, source_target_pairs={{0,16},{16,32},{32,48},{48,64},{64,80},{80,96},{96,112},{112,128},... | collective-permute-start | bytes 9830408 | tf_op jit(solution)/shard_map/ppermute | solution.py:16
  367.2 40.0 %collective-permute-start.3 = (f32[2,100,32,128]{3,2,1,0:T(8,128)S(1)}, f32[2,100,32,128]{3,2,1,0:T(8,128)S(1)}, u32[]{:S(2)}, u32[]{:S(2)}) collective-permute-start(f32[2,100,32,128]{3,2,1,0:T(8,128)S(1)} %fusion.20), channel_id=1, source_target_pairs={{16,0},{32,16},{48,32},{64,48},{80,64},{96,80},{112,96},{128,112},... | collective-permute-start | bytes 9830408 | tf_op jit(solution)/shard_map/ppermute | solution.py:19
  407.2 8.0 %copy-start.1 = (f32[2,100,32,128]{3,2,1,0:T(8,128)S(1)}, f32[2,100,32,128]{3,2,1,0:T(8,128)}, u32[]{:S(2)}) copy-start(f32[2,100,32,128]{3,2,1,0:T(8,128)} %param.5) | copy-start | bytes 9830404
where the time goes:
time: 422 us; the launch traced here: 416 us
  local copies, waits for them, and re-layouts  131 us (31%)
  waiting for transfers between devices  126 us (30%)
  starting transfers between devices  86.6 us (21%)
  matrix products  41.1 us (10%)
  other arithmetic  30.3 us (7%)
    ppermute x2, waiting for transfers between devices, extended(): lax.ppermute(lax.slice_in_dim(block, block.shape[dim] - width, None, axis...  66.9 us
    ppermute x2, starting transfers between devices, extended(): lax.ppermute(lax.slice_in_dim(block, block.shape[dim] - width, None, axis...  66.4 us
    gather x4, local copies, waits for them, and re-layouts, reorder_cells(): reordered = jnp.take(flattened, positions, axis=0)  54.4 us
    all_to_all x1, waiting for transfers between devices, on_device(): lax.all_to_all(picked, 'member', split_axis=2, concat_axis=0, tiled=True)  54.1 us
    dot_general x2, matrix products, band_rows(): jnp.einsum('rp,mvpk->mvrk', lat_band, padded, precision=lax.Precision.HIG...  19 us
    scatter x1, local copies, waits for them, and re-layouts, on_device(): jnp.zeros((mesh_locations,), jnp.int32).at[order]  15.7 us
    unnamed x24, local copies, waits for them, and re-layouts  14.1 us
    all_to_all x1, starting transfers between devices, on_device(): lax.all_to_all(picked, 'member', split_axis=2, concat_axis=0, tiled=True)  11.4 us
  transfers between devices with their start and end apart: 6, of which 5 were waited for; matrix products, arithmetic and copies ran while one was open for 11% of the time, Pallas kernels for 0%

commit v1 on v0

--- a/solution.py
+++ b/solution.py
@@ -69,7 +69,12 @@
         "vkmn,nvkp->mvkp", pair_weights, gathered, precision=lax.Precision.HIGHEST
     )
     apart = apart / members
-    return lax.all_to_all(apart, "member", split_axis=0, concat_axis=2, tiled=True)
+    return jnp.concatenate(
+        lax.all_to_all(
+            jnp.stack(jnp.split(apart, lax.axis_size("member"), axis=0)), "member", 0, 0
+        ),
+        axis=2,
+    )
 
 
 def reorder_cells(values, positions):

time: 422 us -> 432 us (1.024)
  the two profiles are of different devices: /device:TPU:1 before, /device:TPU:107 now
where the time goes in v1:
time: 432 us; the launch traced here: 426 us
  waiting for transfers between devices  181 us (42%)
  local copies, waits for them, and re-layouts  144 us (33%)
  matrix products  41.4 us (10%)
  other arithmetic  30.3 us (7%)
  starting transfers between devices  29.1 us (7%)
    all_to_all x1, waiting for transfers between devices, on_device(): lax.all_to_all(picked, 'member', split_axis=2, concat_axis=0, tiled=True)  75.6 us
    gather x4, local copies, waits for them, and re-layouts, reorder_cells(): reordered = jnp.take(flattened, positions, axis=0)  54.7 us
    ppermute x2, waiting for transfers between devices, extended(): lax.ppermute(lax.slice_in_dim(block, block.shape[dim] - width, None, axis...  50.9 us
    all_to_all x1, waiting for transfers between devices, pair_terms(): lax.all_to_all(jnp.stack(jnp.split(apart, lax.axis_size('member'), axis=0...  49.7 us
    unnamed x39, local copies, waits for them, and re-layouts  26 us
    dot_general x2, matrix products, band_rows(): jnp.einsum('rp,mvpk->mvrk', lat_band, padded, precision=lax.Precision.HIG...  19 us
    scatter x1, local copies, waits for them, and re-layouts, on_device(): jnp.zeros((mesh_locations,), jnp.int32).at[order]  16.1 us
    all_to_all x1, starting transfers between devices, on_device(): lax.all_to_all(picked, 'member', split_axis=2, concat_axis=0, tiled=True)  9.38 us
  transfers between devices with their start and end apart: 6, of which 5 were waited for; matrix products, arithmetic and copies ran while one was open for 11% of the time, Pallas kernels for 0%

profile of v1, /device:TPU:107, one launch (start us, length us, event | category | flops | bytes accessed | tf_op | source)
XLA Modules:
  0.0 425.6 jit_solution(4941373419926805850)
XLA Ops:
  0.6 1.3 copy-done
  1.9 5.9 %fusion.14 = f32[2,100,32,128]{3,1,2,0:T(8,128)S(1)} fusion(f32[2,100,32,128]{3,2,1,0:T(8,128)S(1)} %copy-done, f32[]{:T(128)} %exponential_reduce_fusion), kind=kOutput, calls=%fused_computation.28 | convolution fusion | flops 1258504192 | bytes 6553604 | tf_op jit(solution)/shard_map/mvrl,lk->mvrk/dot_general | solution.py:50
  7.8 0.6 copy.62
  8.5 1.2 copy-done.2
  9.6 3.7 collective-permute-start
  13.3 1.9 collective-permute-start.1
  15.3 16.1 %scatter_custom_fusion = s32[4096]{0:T(1024)S(1)} fusion(s32[4096]{0:T(1024)S(1)} %bitcast.165, s32[4096]{0:T(1024)S(1)} %iota.49, s32[]{:T(128)} %constant.26.clone.1), kind=kCustom, calls=%fused_computation.84 | custom fusion | bytes 16388 | tf_op jit(solution)/shard_map/scatter | solution.py:94
  31.4 17.5 %collective-permute-done = f32[2,100,32,128]{3,2,1,0:T(8,128)} collective-permute-done((f32[2,100,32,128]{3,2,1,0:T(8,128)S(1)}, f32[2,100,32,128]{3,2,1,0:T(8,128)}, u32[]{:S(2)}, u32[]{:S(2)}) %collective-permute-start) | collective-permute-done | bytes 3276832 | tf_op jit(solution)/shard_map/ppermute | solution.py:16
  48.9 5.5 %copy.64 = f32[2,100,32,128]{3,1,2,0:T(8,128)} copy(f32[2,100,32,128]{3,2,1,0:T(8,128)} %collective-permute-done) | data formatting | bytes 6553600 | tf_op jit(solution)/shard_map/ppermute | solution.py:16
  54.4 5.5 %copy.65 = f32[2,100,32,128]{3,1,2,0:T(8,128)} copy(f32[2,100,32,128]{3,2,1,0:T(8,128)} %collective-permute-done.1) | data formatting | bytes 6553600 | tf_op jit(solution)/shard_map/ppermute | solution.py:19
  60.0 8.5 %pad_maximum_fusion = f32[2,100,96,128]{3,1,2,0:T(8,128)} fusion(f32[2,100,32,128]{3,1,2,0:T(8,128)} %copy.65, f32[2,100,32,128]{3,1,2,0:T(8,128)} %copy-done.2, f32[2,100,32,128]{3,1,2,0:T(8,128)} %copy.64), kind=kLoop, calls=%fused_computation.4 | loop fusion | flops 4915200 | bytes 19660800 | tf_op jit(solution)/shard_map/concatenate | solution.py:20
  68.5 10.9 %fusion.6 = f32[2,100,128,32]{2,3,1,0:T(8,128)S(1)} fusion(f32[2,100,96,128]{3,1,2,0:T(8,128)} %pad_maximum_fusion, f32[]{:T(128)} %exponential_reduce_fusion, s32[96]{0:T(128)S(1)} %iota_add_fusion), kind=kOutput, calls=%fused_computation.11 | convolution fusion | flops 943758336 | bytes 13107588 | tf_op jit(solution)/shard_map/rp,mvpk->mvrk/dot_general | solution.py:46
  79.4 2.9 copy.100
  82.2 3.3 copy.67
  85.6 18.4 %gather_fusion.1 = f32[4096,200]{1,0:T(8,128)} fusion(f32[4096,200]{1,0:T(8,128)} %bitcast.147, s32[4096]{0:T(1024)S(1)} %get-tuple-element.8), kind=kCustom, calls=%fused_computation.clone | custom fusion | bytes 6569984 | tf_op jit(solution)/shard_map/jit(_take)/gather | solution.py:83
  104.0 3.7 copy.68
  107.7 1.7 copy-done.5
  110.2 4.2 copy.71
  114.5 9.4 %all-to-all-start = ((f32[2,100,32,128]{3,0,1,2:T(2,128)}), f32[2,100,32,128]{3,0,1,2:T(2,128)S(1)}, u32[]{:S(2)}, u32[]{:S(2)}) async-start(f32[2,100,32,128]{3,0,1,2:T(2,128)} %copy.71), calls=%async_computation | async-start | bytes 6553600 | tf_op jit(solution)/shard_map/all_to_all | solution.py:106
  123.9 75.6 %all-to-all-done = f32[2,100,32,128]{3,0,1,2:T(2,128)S(1)} async-done(((f32[2,100,32,128]{3,0,1,2:T(2,128)}), f32[2,100,32,128]{3,0,1,2:T(2,128)S(1)}, u32[]{:S(2)}, u32[]{:S(2)}) %all-to-all-start) | async-done | bytes 3276832 | tf_op jit(solution)/shard_map/all_to_all | solution.py:106
  199.5 0.6 copy.72
  200.1 3.1 copy.73
  203.3 1.1 multiply_reduce_fusion
  204.3 6.2 %fusion.62 = (f32[100,2,32]{2,1,0:T(2,128)S(1)}, f32[100,2,32,32]{2,3,1,0:T(8,128)S(1)}) fusion(f32[32,100,2,128]{3,0,2,1:T(8,128)S(1)} %bitcast.150, f32[100,2,32]{2,1,0:T(2,128)S(1)} %multiply_reduce_fusion, pred[32,32]{0,1:T(8,128)(4,1)S(1)} %iota_compare_fusion), kind=kOutput, calls=%fused_computation.105 | convolution fusion | flops 316000000 | bytes 4148224 | tf_op jit(solution)/shard_map/mvkp,nvkp->vkmn/dot_general | solution.py:56
  210.6 6.9 %fusion.13 = f32[32,100,2,128]{3,0,2,1:T(8,128)S(1)} fusion(f32[32,100,2,128]{3,0,2,1:T(8,128)S(1)} %bitcast.151, f32[100,2,32,32]{2,3,1,0:T(8,128)S(1)} %get-tuple-element.7, f32[32,100,2]{0,2,1:T(2,128)S(1)} %bitcast.162), kind=kOutput, calls=%fused_computation.23 | convolution fusion | flops 317030400 | bytes 7398400 | tf_op jit(solution)/shard_map/vkmn,nvkp->mvkp/dot_general | solution.py:68
  217.5 0.8 fusion.35
  218.2 0.8 fusion.34
  219.0 0.8 fusion.33
  219.8 0.8 fusion.32
  220.6 0.8 fusion.31
  221.4 0.8 fusion.30
  222.2 0.8 fusion.29
  223.0 0.8 fusion.28
  223.8 0.8 fusion.27
  224.6 0.8 fusion.26
  225.4 0.8 fusion.25
  226.1 0.8 fusion.24
  226.9 0.8 fusion.23
  227.7 0.8 fusion.22
  228.5 0.8 fusion.21
  229.3 0.8 fusion.20
  230.1 8.0 %all-to-all-start.1 = ((f32[16,2,100,2,128]{4,1,3,2,0:T(2,128)}), f32[16,2,100,2,128]{4,1,3,2,0:T(2,128)}, u32[]{:S(2)}, u32[]{:S(2)}) async-start(f32[16,2,100,2,128]{4,1,3,2,0:T(2,128)} %fusion.20), calls=%async_computation.1 | async-start | bytes 6553600 | tf_op jit(solution)/shard_map/all_to_all | solution.py:73
  238.1 1.9 copy.69
  240.0 14.2 %gather_fusion = f32[4096,100]{1,0:T(8,128)} fusion(f32[4096,100]{1,0:T(8,128)S(1)} %bitcast.148, s32[4096]{0:T(1024)S(1)} %broadcast_clamp_fusion), kind=kCustom, calls=%fused_computation.2 | custom fusion | bytes 3293184 | tf_op jit(solution)/shard_map/jit(_take)/gather | solution.py:83
  254.2 4.8 %broadcast_select_fusion = f32[4096,100]{1,0:T(8,128)} fusion(f32[4096,100]{1,0:T(8,128)} %gather_fusion, pred[4096]{0:T(1024)(128)(4,1)S(1)} %compare_and_fusion.1), kind=kLoop, calls=%fused_computation.30 | loop fusion | flops 409600 | bytes 3280896 | tf_op jit(solution)/shard_map/jit(_take)/select_n | solution.py:83
  259.0 3.2 copy.70
  262.2 2.4 multiply_reduce_fusion.1
  264.6 49.7 %all-to-all-done.1 = f32[16,2,100,2,128]{4,1,3,2,0:T(2,128)} async-done(((f32[16,2,100,2,128]{4,1,3,2,0:T(2,128)}), f32[16,2,100,2,128]{4,1,3,2,0:T(2,128)}, u32[]{:S(2)}, u32[]{:S(2)}) %all-to-all-start.1) | async-done | bytes 3276832 | tf_op jit(solution)/shard_map/all_to_all | solution.py:73
  314.3 3.6 copy.75
  318.0 4.3 %reshape.80 = f32[200,4096]{1,0:T(8,128)} reshape(f32[2,100,16,2,128]{4,3,2,1,0:T(2,128)S(1)} %copy.75) | data formatting | bytes 6553600 | tf_op jit(solution)/shard_map/reshape | solution.py:72
  322.3 0.9 div.56
  324.7 1.2 copy-done.6
  325.9 8.6 %fusion.12 = f32[4096,200]{0,1:T(8,128)} fusion(f32[200,4096]{1,0:T(8,128)S(1)} %copy-done.8, f32[25,8,32,128]{3,2,1,0:T(8,128)S(1)} %bitcast.158, f32[25,8,32,128]{3,2,1,0:T(8,128)S(1)} %bitcast.159, f32[4096,200]{0,1:T(8,128)S(1)} %copy-done.6, pred[4096]{0:T(1024)(128)(4,1)S(1)} %compare_and_fusion.1), kind=kLoop, calls=%fused_computation.19 | loop fusion | flops 4096000 | bytes 16388096 | tf_op jit(solution)/shard_map/transpose | solution.py:82
  334.5 5.2 %copy.76 = f32[4096,200]{1,0:T(8,128)} copy(f32[4096,200]{0,1:T(8,128)} %fusion.12) | data formatting | bytes 6553600 | tf_op jit(solution)/shard_map/transpose | solution.py:82
  339.7 18.4 %gather_fusion.2 = f32[4096,200]{1,0:T(8,128)} fusion(f32[4096,200]{1,0:T(8,128)} %copy.76, s32[4096]{0:T(1024)S(1)} %get-tuple-element.9), kind=kCustom, calls=%fused_computation.1.clone | custom fusion | bytes 6569984 | tf_op jit(solution)/shard_map/jit(_take)/gather | solution.py:83
  358.1 3.9 select_bitcast_fusion
  362.0 5.3 %copy.77 = f32[200,4096]{1,0:T(8,128)} copy(f32[200,4096]{0,1:T(8,128)} %select_bitcast_fusion) | data formatting | bytes 6553600 | tf_op jit(solution)/shard_map/transpose | solution.py:84
  367.3 2.5 copy.90
  369.8 3.5 fusion.36
  373.3 3.9 collective-permute-start.2
  377.3 2.2 collective-permute-start.3
  379.5 33.4 %collective-permute-done.2 = f32[2,100,32,128]{3,2,1,0:T(8,128)S(1)} collective-permute-done((f32[2,100,32,128]{3,2,1,0:T(8,128)S(1)}, f32[2,100,32,128]{3,2,1,0:T(8,128)S(1)}, u32[]{:S(2)}, u32[]{:S(2)}) %collective-permute-start.2) | collective-permute-done | bytes 3276832 | tf_op jit(solution)/shard_map/ppermute | solution.py:16
  412.9 4.4 %collective-permute-done.3 = f32[2,100,32,128]{3,2,1,0:T(8,128)S(1)} collective-permute-done((f32[2,100,32,128]{3,2,1,0:T(8,128)S(1)}, f32[2,100,32,128]{3,2,1,0:T(8,128)S(1)}, u32[]{:S(2)}, u32[]{:S(2)}) %collective-permute-start.3) | collective-permute-done | bytes 3276832 | tf_op jit(solution)/shard_map/ppermute | solution.py:19
  417.3 8.1 %fusion.17 = f32[2,100,32,128]{3,2,1,0:T(8,128)} fusion(f32[2,100,32,128]{3,2,1,0:T(8,128)S(1)} %collective-permute-done.3, f32[2,100,32,128]{3,2,1,0:T(8,128)S(1)} %fusion.36, f32[2,100,32,128]{3,2,1,0:T(8,128)S(1)} %collective-permute-done.2, f32[]{:T(128)} %exponential_reduce_fusion, s32[96]{0:T(128)S(1)} %iota_add_fusion), kind=kOutput, calls=%fused_computation.29 | convolution fusion | flops 948673536 | bytes 13107588 | tf_op jit(solution)/shard_map/rp,mvpk->mvrk/dot_general | solution.py:46
  (30 shorter events, 3.1 us)
Async XLA Ops:
  0.0 1.9 copy-start
  7.8 1.8 copy-start.2
  7.8 7.4 %copy-start.9 = (s32[1,4096]{1,0:T(1,128)S(1)}, s32[1,4096]{1,0:T(1,128)}, u32[]{:S(2)}) copy-start(s32[1,4096]{1,0:T(1,128)} %param.7) | copy-start | bytes 49156
  9.6 39.3 %collective-permute-start = (f32[2,100,32,128]{3,2,1,0:T(8,128)S(1)}, f32[2,100,32,128]{3,2,1,0:T(8,128)}, u32[]{:S(2)}, u32[]{:S(2)}) collective-permute-start(f32[2,100,32,128]{3,2,1,0:T(8,128)S(1)} %copy.62), channel_id=1, source_target_pairs={{0,16},{16,32},{32,48},{48,64},{64,80},{80,96},{96,112},{112,128},... | collective-permute-start | bytes 9830408 | tf_op jit(solution)/shard_map/ppermute | solution.py:16
  13.3 41.1 %collective-permute-start.1 = (f32[2,100,32,128]{3,2,1,0:T(8,128)S(1)}, f32[2,100,32,128]{3,2,1,0:T(8,128)}, u32[]{:S(2)}, u32[]{:S(2)}) collective-permute-start(f32[2,100,32,128]{3,2,1,0:T(8,128)S(1)} %copy.62), channel_id=1, source_target_pairs={{16,0},{32,16},{48,32},{64,48},{80,64},{96,80},{112,96},{128,112},... | collective-permute-start | bytes 9830408 | tf_op jit(solution)/shard_map/ppermute | solution.py:19
  107.7 1.7 copy-start.5
  110.2 4.2 copy-start.3
  114.5 85.0 %all-to-all-start = ((f32[2,100,32,128]{3,0,1,2:T(2,128)}), f32[2,100,32,128]{3,0,1,2:T(2,128)S(1)}, u32[]{:S(2)}, u32[]{:S(2)}) async-start(f32[2,100,32,128]{3,0,1,2:T(2,128)} %copy.71), calls=%async_computation | async-start | bytes 6553600 | tf_op jit(solution)/shard_map/all_to_all | solution.py:106
  230.1 84.2 %all-to-all-start.1 = ((f32[16,2,100,2,128]{4,1,3,2,0:T(2,128)}), f32[16,2,100,2,128]{4,1,3,2,0:T(2,128)}, u32[]{:S(2)}, u32[]{:S(2)}) async-start(f32[16,2,100,2,128]{4,1,3,2,0:T(2,128)} %fusion.20), calls=%async_computation.1 | async-start | bytes 6553600 | tf_op jit(solution)/shard_map/all_to_all | solution.py:73
  254.2 8.0 %copy-start.4 = (f32[25,8,32,128]{3,2,1,0:T(8,128)S(1)}, f32[25,8,32,128]{3,2,1,0:T(8,128)}, u32[]{:S(2)}) copy-start(f32[25,8,32,128]{3,2,1,0:T(8,128)} %copy-done.3) | copy-start | bytes 9830404
  322.3 1.4 copy-start.7
  322.3 2.4 copy-start.8
  323.2 2.7 copy-start.6
  373.3 39.5 %collective-permute-start.2 = (f32[2,100,32,128]{3,2,1,0:T(8,128)S(1)}, f32[2,100,32,128]{3,2,1,0:T(8,128)S(1)}, u32[]{:S(2)}, u32[]{:S(2)}) collective-permute-start(f32[2,100,32,128]{3,2,1,0:T(8,128)S(1)} %fusion.36), channel_id=1, source_target_pairs={{0,16},{16,32},{32,48},{48,64},{64,80},{80,96},{96,112},{112,128},... | collective-permute-start | bytes 9830408 | tf_op jit(solution)/shard_map/ppermute | solution.py:16
  377.3 40.0 %collective-permute-start.3 = (f32[2,100,32,128]{3,2,1,0:T(8,128)S(1)}, f32[2,100,32,128]{3,2,1,0:T(8,128)S(1)}, u32[]{:S(2)}, u32[]{:S(2)}) collective-permute-start(f32[2,100,32,128]{3,2,1,0:T(8,128)S(1)} %fusion.36), channel_id=1, source_target_pairs={{16,0},{32,16},{48,32},{64,48},{80,64},{96,80},{112,96},{128,112},... | collective-permute-start | bytes 9830408 | tf_op jit(solution)/shard_map/ppermute | solution.py:19
  417.3 8.1 %copy-start.1 = (f32[2,100,32,128]{3,2,1,0:T(8,128)S(1)}, f32[2,100,32,128]{3,2,1,0:T(8,128)}, u32[]{:S(2)}) copy-start(f32[2,100,32,128]{3,2,1,0:T(8,128)} %param.5) | copy-start | bytes 9830404
